TPU v7x, 32 devices: a whole 2x2x4 slice. The times are simulated.
32 devices in a mesh: groups: 2 (over y), blk: 4 (over z), win: 4 (over x, core).
Axes of the slice: x: 2, y: 2, z: 4, core: 2. Of those that a mesh axis runs over, the one named last changes fastest.
Arguments:
- spectra: bfloat16 [2, 24, 1024, 201], P(None, 'win', ('groups', 'blk')), parts along dimension 2
- channel_slot: int32 [1024], P(('groups', 'blk')), parts along dimension 0, may hold values from 0 to 511, as said below
- partners: int32 [2, 4], replicated, may hold values from 0 to 3, as said below
Outputs:
- correlations: bfloat16 [2, 1024, 101, 128], P(None, ('groups', 'blk', 'win')), parts along dimension 1
There are 2 independent parts, one for each index of `groups`. A program takes and returns all parts, laid end to end along the dimension named above; an argument that names none is the same for every part. Nothing has to cross between parts.
Inputs may be any that keep to these rules, and one draw needn't show every extreme that they name: channel_slot is a permutation of 0 to 511. For every acquisition shard s (channels s * 128 to s * 128 + 127) and every block b, exactly 32 of the shard's channels go to block b, and they take the slots b * 128 + s * 32 + q for q from 0 to 31. In round r, partners[r, i] = i XOR m_r for one value m_r of 1 to 3 per round; the rounds' values differ.
All inputs are finite; a program needn't handle non-finite values.
Results may differ from a plain program's by a relative error of at most 0.0057.
Values may be sent and summed in bfloat16 or wider, within the bound.
A program may use at most 128 MiB of HBM per device.

v0:
```python
import functools
import math

import jax
import jax.numpy as jnp
from jax import lax
from jax.experimental import pallas as pl
from jax.experimental.pallas import tpu as pltpu
from jax.sharding import PartitionSpec as P

L = 101
ROUNDS = 2


eps_power = 1e-06
half_band = 2
tile_rows = 8


def band_mean(power, windows):
    nbins = power.shape[1]
    padded = jnp.pad(power, ((0, 0), (half_band, half_band)))
    ones = jnp.pad(jnp.ones((nbins,), jnp.float32), (half_band, half_band))
    total = padded[:, 0:nbins]
    count = ones[0:nbins]
    for offset in range(1, 2 * half_band + 1):
        total = total + padded[:, offset : offset + nbins]
        count = count + ones[offset : offset + nbins]
    return total / (count * windows)


def whiten(parts, power, windows):
    scale = lax.rsqrt(band_mean(power, windows) + eps_power)
    return (parts.astype(jnp.float32) * scale).astype(jnp.bfloat16)


def lag_table(nbins, nlags, windows):
    samples = 2 * (nbins - 1)
    freq = jnp.arange(nbins, dtype=jnp.int32)
    lags = jnp.arange(nlags, dtype=jnp.int32) - (nlags - 1) // 2
    phase_index = freq[:, None] * lags[None, :] % samples
    angle = 2.0 * math.pi / samples * phase_index.astype(jnp.float32)
    weight = jnp.where((freq == 0) | (freq == nbins - 1), 1.0, 2.0).astype(jnp.float32)
    norm = 1.0 / math.sqrt(windows * samples)
    cos_part = weight[:, None] * jnp.cos(angle) * norm
    sin_part = -weight[:, None] * jnp.sin(angle) * norm
    return jnp.concatenate([cos_part, sin_part], axis=0)


def correlate(both, right, table):
    cross = jnp.einsum(
        "wcak,wbk->kcab", both, right, preferred_element_type=jnp.float32
    ).astype(jnp.bfloat16)
    return jnp.einsum(
        "kcab,ckl->alb", cross, table, preferred_element_type=jnp.float32
    ).astype(jnp.bfloat16)


def whiten_all(parts, windows):
    value_array = parts.astype(jnp.float32)
    power = jnp.sum(value_array * value_array, axis=0)
    return whiten(parts, power, windows)


def flip(index, bit):
    return index + bit - 2 * bit * ((index // bit) % 2)


def exchange_kernel(
    n_blk, n_win, pair_ref, own_ref, got_ref, src_ref, pair_stage, own_stage,
    pair_send, pair_recv, pass_send, pass_recv, own_send, own_recv, local_sem
):
    blk = lax.axis_index("blk")
    win = lax.axis_index("win")
    per_share = n_blk // n_win
    barrier = pltpu.get_barrier_semaphore()
    for step in range(1, n_blk * n_win):
        other = (blk * n_win + win + step) % (n_blk * n_win)
        pl.semaphore_signal(
            barrier,
            inc=1,
            device_id={"blk": other // n_win, "win": other % n_win},
            device_id_type=pl.DeviceIdType.MESH,
        )
    pl.semaphore_wait(barrier, n_blk * n_win - 1)

    def remote(src, dst, send, recv, to_blk, to_win):
        return pltpu.make_async_remote_copy(
            src_ref=src,
            dst_ref=dst,
            send_sem=send,
            recv_sem=recv,
            device_id={"blk": to_blk, "win": to_win},
            device_id_type=pl.DeviceIdType.MESH,
        )

    bits = []
    bit = n_win // 2
    while bit:
        bits.append(bit)
        bit //= 2

    def direct(step):
        dest = (blk + step) % n_blk
        return remote(
            pair_ref.at[:, :, dest], got_ref.at[:, win, :, blk],
            pair_send.at[step], pair_recv.at[step], dest, win,
        )

    user = blk // per_share
    place = blk % per_share

    def own(step):
        dest = (blk + step) % n_blk
        return remote(
            own_ref.at[:, dest], src_ref.at[win, :, place],
            own_send.at[step], own_recv.at[place * n_win + win], dest, user,
        )

    def passed(step, offset, over):
        origin = (blk + n_blk - step) % n_blk
        slot = win
        for each in bits:
            if offset & each:
                slot = flip(slot, each)
        target = got_ref.at[:, slot, :, origin]
        source = pair_ref.at[:, :, blk] if step == 0 and offset == 0 else target
        mark = (offset | over) - 1
        return remote(
            source, target, pass_send.at[mark, step], pass_recv.at[mark, step], blk, flip(win, over)
        )

    stage_in = pltpu.make_async_copy(pair_ref.at[:, :, blk], pair_stage, local_sem.at[0])
    stage_in.start()
    is_user = user == win

    def own_in():
        return pltpu.make_async_copy(own_ref.at[:, blk], own_stage, local_sem.at[1])

    def own_out():
        return pltpu.make_async_copy(own_stage, src_ref.at[win, :, place], local_sem.at[2])

    @pl.when(is_user)
    def _():
        own_in().start()

    passes = []
    held = [0]
    for over in bits:
        passes.extend((offset, over) for offset in held)
        held = held + [offset | over for offset in held]

    sends = []
    for offset, over in passes:
        if offset == 0:
            copy = passed(0, 0, over)
            copy.start()
            sends.append(copy)
    for step in range(1, n_blk):
        copy = direct(step)
        copy.start()
        sends.append(copy)
    for step in range(1, n_blk):
        copy = own(step)
        copy.start()
        sends.append(copy)

    @pl.when(jnp.logical_not(is_user))
    def _():
        own(0).start()

    stage_in.wait()
    stage_out = pltpu.make_async_copy(pair_stage, got_ref.at[:, win, :, blk], local_sem.at[3])
    stage_out.start()

    @pl.when(is_user)
    def _():
        own_in().wait()
        own_out().start()

    waited = set()

    def arrive(step, offset):
        if (step, offset) in waited:
            return
        waited.add((step, offset))
        if offset == 0:
            if step:
                direct(step).wait_recv()
        else:
            over = offset & -offset
            passed(step, offset - over, over).wait_recv()

    for step in range(n_blk + 1):
        if 1 <= step < n_blk:
            arrive(step, 0)
            for offset, over in passes:
                if offset == 0:
                    copy = passed(step, 0, over)
                    copy.start()
                    sends.append(copy)
        if step >= 1:
            for offset, over in passes:
                if offset:
                    arrive(step - 1, offset)
                    copy = passed(step - 1, offset, over)
                    copy.start()
                    sends.append(copy)
    for step in range(n_blk):
        for offset in held:
            arrive(step, offset)

    for local in range(per_share):
        for peer in range(n_win):
            here = jnp.logical_and(blk == win * per_share + local, win == peer)

            @pl.when(jnp.logical_not(here))
            def _():
                piece = src_ref.at[peer, :, local]
                remote(
                    piece, piece, own_send.at[0], own_recv.at[local * n_win + peer], blk, win
                ).wait_recv()

    for copy in sends:
        copy.wait_send()

    @pl.when(jnp.logical_not(is_user))
    def _():
        own(0).wait_send()

    stage_out.wait()

    @pl.when(is_user)
    def _():
        own_out().wait()


def exchange(pair, own, n_blk, n_win):
    rounds, rows, _, per_peer, nbins = pair.shape
    per_share = n_blk // n_win
    dtype = pair.dtype
    anywhere = pl.BlockSpec(memory_space=pl.ANY)
    return pl.pallas_call(
        functools.partial(exchange_kernel, n_blk, n_win),
        out_shape=(
            jax.ShapeDtypeStruct((rounds, n_win, rows, n_blk, per_peer, nbins), dtype),
            jax.ShapeDtypeStruct((n_win, rows, per_share, per_peer, nbins), dtype),
        ),
        in_specs=[anywhere, anywhere],
        out_specs=(anywhere, anywhere),
        scratch_shapes=[
            pltpu.VMEM((rounds, rows, per_peer, nbins), dtype),
            pltpu.VMEM((rows, per_peer, nbins), dtype),
            pltpu.SemaphoreType.DMA((n_blk,)),
            pltpu.SemaphoreType.DMA((n_blk,)),
            pltpu.SemaphoreType.DMA((n_win - 1, n_blk)),
            pltpu.SemaphoreType.DMA((n_win - 1, n_blk)),
            pltpu.SemaphoreType.DMA((n_blk,)),
            pltpu.SemaphoreType.DMA((n_blk,)),
            pltpu.SemaphoreType.DMA((4,)),
        ],
        compiler_params=pltpu.CompilerParams(collective_id=0, has_side_effects=True),
    )(pair, own)


def body(spectra, channel_slot, partners):
    n_blk = lax.axis_size("blk")
    n_win = lax.axis_size("win")
    parts, mine, chans, nbins = spectra.shape
    rows = parts * mine
    per_peer = chans // n_blk
    here = lax.axis_index("blk")
    share = chans // n_win
    windows = mine * n_win
    flat = spectra.reshape(rows, chans, nbins)
    wanted = jnp.concatenate([partners, jnp.arange(n_blk, dtype=jnp.int32)[None]], axis=0)
    slots = (
        wanted[:, :, None] * chans
        + here * per_peer
        + jnp.arange(per_peer, dtype=jnp.int32)[None, None, :]
    )
    selector = (slots[..., None] == channel_slot).astype(jnp.bfloat16)
    pair = jnp.einsum(
        "tzqc,xcf->txzqf", selector[:ROUNDS], flat, preferred_element_type=jnp.float32
    ).astype(jnp.bfloat16)
    own = jnp.einsum(
        "zqc,xcf->xzqf", selector[ROUNDS], flat, preferred_element_type=jnp.float32
    ).astype(jnp.bfloat16)
    got, mine_all = exchange(pair, own, n_blk, n_win)
    sources = whiten_all(mine_all.reshape(n_win * rows, share, nbins), windows)
    split = sources.reshape(n_win, parts, mine, share, nbins)
    turned = jnp.stack([split[:, 1], -split[:, 0]], axis=1).reshape(sources.shape)
    both = jnp.stack([sources, turned], axis=1)
    table = lag_table(nbins, L, windows).reshape(2, nbins, L).astype(jnp.bfloat16)
    results = []
    for round_index in range(ROUNDS):
        right = got[round_index].reshape(n_win * rows, chans, nbins)
        results.append(correlate(both, whiten_all(right, windows), table))
    return jnp.stack(results, axis=0)


def solution(mesh):
    in_specs = (P(None, "win", ("groups", "blk"), None), P(("groups", "blk")), P())
    out_specs = P(None, ("groups", "blk", "win"), None, None)
    return jax.shard_map(body, mesh=mesh, in_specs=in_specs, out_specs=out_specs, check_vma=False)
```

profile of v0, /device:TPU:25, one launch (start us, length us, event | category | flops | bytes accessed | tf_op | source)
XLA Modules:
  0.0 133.9 jit_solution(11599635203869048731)
XLA Ops:
  0.0 1.2 copy.7
  1.2 0.7 fusion.16
  1.9 0.1 iota_add_fusion
  1.9 0.8 broadcast_compare_fusion
  2.7 1.7 %fusion.5.pair_ref = bf16[2,12,4,32,201]{4,3,2,1,0:T(8,128)(2,1)} fusion(bf16[12,128,201,1,1]{1,2,4,0,3:T(8,128)(2,1)S(1)} %bitcast.71, pred[3,4,32,128]{3,2,1,0:T(32,128)(4,1)S(1)} %broadcast_compare_fusion), kind=kOutput, calls=%fused_computation.21 | convolution fusion | flops 158690304 | bytes 1906688 | tf_op jit(solution)/shard_map/tzqc,xcf->txzqf/dot_general | solution.py:283
  4.5 1.5 %fusion.8.own_ref = bf16[12,4,32,201]{3,2,1,0:T(8,128)(2,1)} fusion(bf16[12,128,201,1]{1,2,3,0:T(8,128)(2,1)S(1)} %bitcast.72, pred[3,4,32,128]{3,2,1,0:T(32,128)(4,1)S(1)} %broadcast_compare_fusion), kind=kOutput, calls=%fused_computation.25 | convolution fusion | flops 79345152 | bytes 1272832 | tf_op jit(solution)/shard_map/zqc,xcf->xzqf/dot_general | solution.py:286
  5.9 72.3 %shard_map.37 = (bf16[2,4,12,4,32,201]{5,4,3,2,1,0:T(8,128)(2,1)}, bf16[4,12,1,32,201]{4,3,2,1,0:T(8,128)(2,1)}) custom-call(bf16[2,12,4,32,201]{4,3,2,1,0:T(8,128)(2,1)} %fusion.5.pair_ref, bf16[12,4,32,201]{3,2,1,0:T(8,128)(2,1)} %fusion.8.own_ref), custom_call_target="tpu_custom_call" | custom-call | tf_op jit(solution)/shard_map/pallas_call | solution.py:243
  78.2 1.3 multiply_reduce_fusion.2
  79.5 0.1 fusion.21
  79.6 0.1 add_rsqrt_fusion.2
  79.7 1.3 convert_element_type.136
  81.1 0.2 fusion.4
  81.3 0.1 fusion.23
  81.3 0.1 pad_maximum_fusion.2
  81.5 0.2 multiply_convert_fusion.2
  81.7 1.4 %pad_maximum_fusion.1 = bf16[48,2,32,201]{3,2,0,1:T(8,128)(2,1)} fusion(bf16[48,1,32,201]{3,2,0,1:T(8,128)(2,1)S(1)} %bitcast.73, bf16[48,1,32,201]{3,2,0,1:T(8,128)(2,1)S(1)} %multiply_convert_fusion.2), kind=kLoop, calls=%fused_computation.16 | loop fusion | flops 617472 | bytes 2469888 | tf_op jit(solution)/shard_map/stack | solution.py:293
  83.2 6.5 %copy.18 = bf16[48,2,32,201]{0,2,1,3:T(8,128)(2,1)S(1)} copy(bf16[48,2,32,201]{3,2,0,1:T(8,128)(2,1)} %pad_maximum_fusion.1) | data formatting | bytes 2469888 | tf_op jit(solution)/shard_map/stack | solution.py:293
  89.7 3.7 %multiply_reduce_fusion.1 = (f32[4,32,201]{2,1,0:T(8,128)S(1)}, f32[4,32,201]{2,1,0:T(8,128)S(1)}) fusion(bf16[2,4,12,4,32,201]{5,4,3,2,1,0:T(8,128)(2,1)} %get-tuple-element.8), kind=kLoop, calls=%fused_computation.5 | loop fusion | flops 7358208 | bytes 5145600 | tf_op jit(solution)/shard_map/reduce_sum | solution.py:61
  93.3 0.3 add_rsqrt_fusion.1
  93.7 7.1 %slice_convert_fusion.1 = (f32[1,4,12,4,32,201]{5,4,3,2,1,0:T(8,128)S(1)}, f32[1,4,12,4,32,201]{5,4,3,2,1,0:T(8,128)}) fusion(bf16[2,4,12,4,32,201]{5,4,3,2,1,0:T(8,128)(2,1)} %get-tuple-element.8), kind=kLoop, calls=%fused_computation.11 | loop fusion | flops 2469888 | bytes 14819328 | tf_op jit(solution)/shard_map/convert_element_type | solution.py:34
  100.8 7.1 %fusion.2 = (bf16[48,128,201,1]{2,1,0,3:T(8,128)(2,1)}, bf16[48,128,201,1]{2,1,0,3:T(8,128)(2,1)}) fusion(f32[48,128,201]{2,1,0:T(8,128)S(1)} %bitcast.67, f32[128,201]{1,0:T(8,128)S(1)} %get-tuple-element.15, f32[48,128,201]{2,1,0:T(8,128)} %bitcast.68, f32[128,201]{1,0:T(8,128)S(1)} %get-tuple-element.16), kind=kLoop, calls=%fused_computation.8 | loop fusion | flops 4939776 | bytes 15025152 | tf_op jit(solution)/shard_map/convert_element_type | solution.py:34
  107.9 4.8 %copy.19 = bf16[48,128,201,1]{1,0,3,2:T(8,128)(2,1)} copy(bf16[48,128,201,1]{2,1,0,3:T(8,128)(2,1)} %get-tuple-element.19) | data formatting | bytes 4939776 | tf_op jit(solution)/shard_map/convert_element_type | solution.py:34
  112.7 4.4 %fusion.24 = bf16[201,2,32,128]{3,2,1,0:T(8,128)(2,1)} fusion(bf16[48,2,32,201]{0,2,1,3:T(8,128)(2,1)S(1)} %copy.18, bf16[48,128,201,1]{1,0,3,2:T(8,128)(2,1)} %copy.19), kind=kOutput, calls=%fused_computation.65 | convolution fusion | flops 158072832 | bytes 6998016 | tf_op jit(solution)/shard_map/wcak,wbk->kcab/dot_general | solution.py:51
  117.1 0.5 multiply_convert_fusion.4
  117.7 5.0 %fusion.6 = bf16[1,32,101,128]{3,2,1,0:T(8,128)(2,1)} fusion(bf16[201,2,32,128]{3,2,1,0:T(8,128)(2,1)} %fusion.24, bf16[2,201,101]{2,1,0:T(8,128)(2,1)S(1)} %convert_element_type.110), kind=kOutput, calls=%fused_computation.23 | convolution fusion | flops 333025280 | bytes 4201780 | tf_op jit(solution)/shard_map/kcab,ckl->alb/dot_general | solution.py:54
  122.6 4.8 %copy.23 = bf16[48,128,201,1]{1,0,3,2:T(8,128)(2,1)} copy(bf16[48,128,201,1]{2,1,0,3:T(8,128)(2,1)} %get-tuple-element.20) | data formatting | bytes 4939776 | tf_op jit(solution)/shard_map/convert_element_type | solution.py:34
  127.4 2.7 %fusion.25 = bf16[201,2,32,128]{3,2,1,0:T(8,128)(2,1)S(1)} fusion(bf16[48,2,32,201]{0,2,1,3:T(8,128)(2,1)S(1)} %copy.18, bf16[48,128,201,1]{1,0,3,2:T(8,128)(2,1)} %copy.23), kind=kOutput, calls=%fused_computation.66 | convolution fusion | flops 158072832 | bytes 6998016 | tf_op jit(solution)/shard_map/wcak,wbk->kcab/dot_general | solution.py:51
  130.1 0.0 copy-start
  130.1 2.1 %fusion.7 = bf16[1,32,101,128]{3,2,1,0:T(8,128)(2,1)S(1)} fusion(bf16[201,2,32,128]{3,2,1,0:T(8,128)(2,1)S(1)} %fusion.25, bf16[2,201,101]{2,1,0:T(8,128)(2,1)S(1)} %convert_element_type.110), kind=kOutput, calls=%fused_computation.24 | convolution fusion | flops 333025280 | bytes 4201780 | tf_op jit(solution)/shard_map/kcab,ckl->alb/dot_general | solution.py:54
  132.3 0.0 copy-done
  132.3 0.2 pad_maximum_fusion
  132.5 1.4 %copy.12 = bf16[2,32,101,128]{3,1,2,0:T(8,128)(2,1)} copy(bf16[2,32,101,128]{3,2,1,0:T(8,128)(2,1)S(1)} %pad_maximum_fusion) | data formatting | bytes 3309568 | tf_op jit(solution)/shard_map/stack | solution.py:299
  (6 shorter events, 0.1 us)
Async XLA Ops:
  130.1 2.2 %copy-start = (bf16[1,32,101,128]{3,2,1,0:T(8,128)(2,1)S(1)}, bf16[1,32,101,128]{3,2,1,0:T(8,128)(2,1)}, u32[]{:S(2)}) copy-start(bf16[1,32,101,128]{3,2,1,0:T(8,128)(2,1)} %fusion.6) | copy-start | bytes 2482180
where the time goes:
time: 134 us
  Pallas kernels  72.3 us (54%)
  other arithmetic  25.3 us (19%)
  local copies, waits for them, and re-layouts  18.8 us (14%)
  matrix products  17.4 us (13%)
    pallas_call x1, Pallas kernels, exchange(): pl.pallas_call(functools.partial(exchange_kernel, n_blk, n_win), out_shap...  72.3 us
    convert_element_type x5, other arithmetic, whiten(): return (parts.astype(jnp.float32) * scale).astype(jnp.bfloat16)  15.9 us
    convert_element_type x2, local copies, waits for them, and re-layouts, whiten(): return (parts.astype(jnp.float32) * scale).astype(jnp.bfloat16)  9.62 us
    dot_general x2, matrix products, correlate(): jnp.einsum('wcak,wbk->kcab', both, right, preferred_element_type=jnp.floa...  7.12 us
    dot_general x2, matrix products, correlate(): jnp.einsum('kcab,ckl->alb', cross, table, preferred_element_type=jnp.floa...  7.1 us
    another operation x1, local copies, waits for them, and re-layouts, body(): both = jnp.stack([sources, turned], axis=1)  6.53 us
    reduce_sum x2, other arithmetic, whiten_all(): power = jnp.sum(value_array * value_array, axis=0)  4.99 us

commit v1 on v0

--- a/solution.py
+++ b/solution.py
@@ -17,21 +17,45 @@
 tile_rows = 8
 
 
-def band_mean(power, windows):
-    nbins = power.shape[1]
-    padded = jnp.pad(power, ((0, 0), (half_band, half_band)))
-    ones = jnp.pad(jnp.ones((nbins,), jnp.float32), (half_band, half_band))
+def whiten_kernel(values_ref, out_ref):
+    n_win, rows, _, _, nbins = values_ref.shape[1:]
+    half = rows // 2
+    power = None
+    for win in range(n_win):
+        value_array = values_ref[0, win, :, 0].astype(jnp.float32)
+        part = jnp.sum(value_array * value_array, axis=0)
+        power = part if power is None else power + part
+    padding = jnp.zeros((power.shape[0], half_band), jnp.float32)
+    padded = jnp.concatenate([padding, power, padding], axis=1)
     total = padded[:, 0:nbins]
-    count = ones[0:nbins]
     for offset in range(1, 2 * half_band + 1):
         total = total + padded[:, offset : offset + nbins]
-        count = count + ones[offset : offset + nbins]
-    return total / (count * windows)
-
-
-def whiten(parts, power, windows):
-    scale = lax.rsqrt(band_mean(power, windows) + eps_power)
-    return (parts.astype(jnp.float32) * scale).astype(jnp.bfloat16)
+    place = lax.broadcasted_iota(jnp.int32, power.shape, 1)
+    count = 1 + jnp.minimum(place, half_band) + jnp.minimum(nbins - 1 - place, half_band)
+    windows = n_win * rows // 2
+    level = total / (count.astype(jnp.float32) * windows)
+    scale = lax.rsqrt(level + eps_power)
+    for win in range(n_win):
+        value_array = values_ref[0, win, :, 0].astype(jnp.float32)
+        white = (value_array * scale).astype(out_ref.dtype)
+        out_ref[0, pl.ds(win * rows, rows), 0] = white
+        if out_ref.shape[0] == 2:
+            out_ref[1, pl.ds(win * rows, half), 0] = white[half:]
+            out_ref[1, pl.ds(win * rows + half, half), 0] = -white[:half]
+
+
+def whiten_all(values, index, forms):
+    _, n_win, rows, shards, per_peer, nbins = values.shape
+    out = pl.pallas_call(
+        whiten_kernel,
+        grid=(shards,),
+        out_shape=jax.ShapeDtypeStruct((forms, n_win * rows, shards, per_peer, nbins), values.dtype),
+        in_specs=[
+            pl.BlockSpec((1, n_win, rows, 1, per_peer, nbins), lambda s: (index, 0, 0, s, 0, 0))
+        ],
+        out_specs=pl.BlockSpec((forms, n_win * rows, 1, per_peer, nbins), lambda s: (0, 0, s, 0, 0)),
+    )(values)
+    return out.reshape(forms, n_win * rows, shards * per_peer, nbins)
 
 
 def lag_table(nbins, nlags, windows):
@@ -49,17 +73,11 @@
 
 def correlate(both, right, table):
     cross = jnp.einsum(
-        "wcak,wbk->kcab", both, right, preferred_element_type=jnp.float32
+        "cwak,wbk->kcab", both, right, preferred_element_type=jnp.float32
     ).astype(jnp.bfloat16)
     return jnp.einsum(
-        "kcab,ckl->alb", cross, table, preferred_element_type=jnp.float32
+        "kcab,ckl->lab", cross, table, preferred_element_type=jnp.float32
     ).astype(jnp.bfloat16)
-
-
-def whiten_all(parts, windows):
-    value_array = parts.astype(jnp.float32)
-    power = jnp.sum(value_array * value_array, axis=0)
-    return whiten(parts, power, windows)
 
 
 def flip(index, bit):
@@ -287,16 +305,12 @@
         "zqc,xcf->xzqf", selector[ROUNDS], flat, preferred_element_type=jnp.float32
     ).astype(jnp.bfloat16)
     got, mine_all = exchange(pair, own, n_blk, n_win)
-    sources = whiten_all(mine_all.reshape(n_win * rows, share, nbins), windows)
-    split = sources.reshape(n_win, parts, mine, share, nbins)
-    turned = jnp.stack([split[:, 1], -split[:, 0]], axis=1).reshape(sources.shape)
-    both = jnp.stack([sources, turned], axis=1)
+    both = whiten_all(mine_all[None], 0, 2)
     table = lag_table(nbins, L, windows).reshape(2, nbins, L).astype(jnp.bfloat16)
-    results = []
-    for round_index in range(ROUNDS):
-        right = got[round_index].reshape(n_win * rows, chans, nbins)
-        results.append(correlate(both, whiten_all(right, windows), table))
-    return jnp.stack(results, axis=0)
+    results = [
+        correlate(both, whiten_all(got, index, 1)[0], table) for index in range(ROUNDS)
+    ]
+    return jnp.stack(results, axis=0).transpose(0, 2, 1, 3)
 
 
 def solution(mesh):

time: 134 us -> 125 us (0.933)
  other arithmetic: 25.3 us -> 2.21 us
  Pallas kernels: 72.3 us -> 85.8 us
    convert_element_type x5 -> x0, other arithmetic: 15.9 us -> none  [whiten(): return (parts.astype(jnp.float32) * scale).astype(jnp.bfloat16)]
    pallas_call x0 -> x3, Pallas kernels: none -> 13.5 us  [whiten_all(): pl.pallas_call(whiten_kernel, grid=(shards,), out_shape=jax.ShapeDtypeStr...]
    convert_element_type x2 -> x0, local copies, waits for them, and re-layouts: 9.62 us -> none  [whiten(): return (parts.astype(jnp.float32) * scale).astype(jnp.bfloat16)]
    reshape x0 -> x1, local copies, waits for them, and re-layouts: none -> 6.53 us  [whiten_all(): return out.reshape(forms, n_win * rows, shards * per_peer, nbins)]
    reduce_sum x2 -> x0, other arithmetic: 4.99 us -> none  [whiten_all(): power = jnp.sum(value_array * value_array, axis=0)]
    another operation x4 -> x1, other arithmetic: 2.21 us -> 0.47 us  [the longest x1 1.45 us: body(): both = jnp.stack([sources, turned], axis=1)]
    another operation x2, local copies, waits for them, and re-layouts: 7.94 us -> 9.57 us  [body(): whiten_all(got, index, 1)[0]]
    transpose x0 -> x1, local copies, waits for them, and re-layouts: none -> 1.41 us  [body(): return jnp.stack(results, axis=0).transpose(0, 2, 1, 3)]
where the time goes in v1:
time: 125 us; the launch traced here: 124 us
  Pallas kernels  85.8 us (69%)
  local copies, waits for them, and re-layouts  18.7 us (15%)
  matrix products  17.4 us (14%)
  other arithmetic  2.21 us (2%)
    pallas_call x1, Pallas kernels, exchange(): pl.pallas_call(functools.partial(exchange_kernel, n_blk, n_win), out_shap...  72.3 us
    pallas_call x3, Pallas kernels, whiten_all(): pl.pallas_call(whiten_kernel, grid=(shards,), out_shape=jax.ShapeDtypeStr...  13.5 us
    another operation x2, local copies, waits for them, and re-layouts, body(): whiten_all(got, index, 1)[0]  9.57 us
    dot_general x2, matrix products, correlate(): jnp.einsum('cwak,wbk->kcab', both, right, preferred_element_type=jnp.floa...  7.13 us
    dot_general x2, matrix products, correlate(): jnp.einsum('kcab,ckl->lab', cross, table, preferred_element_type=jnp.floa...  7.1 us
    reshape x1, local copies, waits for them, and re-layouts, whiten_all(): return out.reshape(forms, n_win * rows, shards * per_peer, nbins)  6.53 us

profile of v1, /device:TPU:25, one launch (start us, length us, event | category | flops | bytes accessed | tf_op | source)
XLA Modules:
  0.0 124.2 jit_solution(17592638109190676929)
XLA Ops:
  0.0 1.2 copy.7
  1.2 0.7 fusion.13
  1.9 0.1 iota_add_fusion
  1.9 0.8 broadcast_compare_fusion
  2.7 1.7 %fusion.2.pair_ref = bf16[2,12,4,32,201]{4,3,2,1,0:T(8,128)(2,1)} fusion(bf16[12,128,201,1,1]{1,2,4,0,3:T(8,128)(2,1)S(1)} %bitcast.61, pred[3,4,32,128]{3,2,1,0:T(32,128)(4,1)S(1)} %broadcast_compare_fusion), kind=kOutput, calls=%fused_computation.8 | convolution fusion | flops 158690304 | bytes 1906688 | tf_op jit(solution)/shard_map/tzqc,xcf->txzqf/dot_general | solution.py:301
  4.5 1.4 %fusion.5.own_ref = bf16[12,4,32,201]{3,2,1,0:T(8,128)(2,1)} fusion(bf16[12,128,201,1]{1,2,3,0:T(8,128)(2,1)S(1)} %bitcast.62, pred[3,4,32,128]{3,2,1,0:T(32,128)(4,1)S(1)} %broadcast_compare_fusion), kind=kOutput, calls=%fused_computation.12 | convolution fusion | flops 79345152 | bytes 1272832 | tf_op jit(solution)/shard_map/zqc,xcf->xzqf/dot_general | solution.py:304
  5.9 72.3 %shard_map.37 = (bf16[2,4,12,4,32,201]{5,4,3,2,1,0:T(8,128)(2,1)}, bf16[4,12,1,32,201]{4,3,2,1,0:T(8,128)(2,1)}) custom-call(bf16[2,12,4,32,201]{4,3,2,1,0:T(8,128)(2,1)} %fusion.2.pair_ref, bf16[12,4,32,201]{3,2,1,0:T(8,128)(2,1)} %fusion.5.own_ref), custom_call_target="tpu_custom_call" | custom-call | tf_op jit(solution)/shard_map/pallas_call | solution.py:261
  78.2 5.3 %shard_map.39 = bf16[1,48,4,32,201]{4,3,2,1,0:T(8,128)(2,1)} custom-call(bf16[2,4,12,4,32,201]{5,4,3,2,1,0:T(8,128)(2,1)} %get-tuple-element.8.values_ref), custom_call_target="tpu_custom_call" | custom-call | tf_op jit(solution)/shard_map/pallas_call | solution.py:49
  83.5 4.8 %copy.19 = bf16[48,128,201,1]{1,0,3,2:T(8,128)(2,1)} copy(bf16[48,128,201,1]{2,1,0,3:T(8,128)(2,1)} %bitcast.59) | data formatting | bytes 4939776 | tf_op jit(solution)/shard_map/squeeze;reshape | solution.py:311
  88.3 2.8 %shard_map.38 = bf16[2,48,1,32,201]{4,3,2,1,0:T(8,128)(2,1)} custom-call(bf16[1,4,12,1,32,201]{5,4,3,2,1,0:T(8,128)(2,1)} %bitcast.63), custom_call_target="tpu_custom_call" | custom-call | tf_op jit(solution)/shard_map/pallas_call | solution.py:49
  91.1 6.5 %copy.18 = bf16[2,48,32,201]{1,2,0,3:T(8,128)(2,1)S(1)} copy(bf16[2,48,32,201]{3,2,1,0:T(8,128)(2,1)} %bitcast.60) | data formatting | bytes 2469888 | tf_op jit(solution)/shard_map/reshape | solution.py:58
  97.6 4.4 %fusion.15 = bf16[201,2,32,128]{3,2,1,0:T(8,128)(2,1)} fusion(bf16[2,48,32,201]{1,2,0,3:T(8,128)(2,1)S(1)} %copy.18, bf16[48,128,201,1]{1,0,3,2:T(8,128)(2,1)} %copy.19), kind=kOutput, calls=%fused_computation.34 | convolution fusion | flops 158072832 | bytes 6998016 | tf_op jit(solution)/shard_map/cwak,wbk->kcab/dot_general | solution.py:75
  102.1 0.5 multiply_convert_fusion.1
  102.6 5.0 %fusion.3 = bf16[1,101,32,128]{3,1,2,0:T(8,128)(2,1)} fusion(bf16[201,2,32,128]{3,2,1,0:T(8,128)(2,1)} %fusion.15, bf16[2,201,101]{2,1,0:T(8,128)(2,1)S(1)} %convert_element_type.33), kind=kOutput, calls=%fused_computation.10 | convolution fusion | flops 333025280 | bytes 4201780 | tf_op jit(solution)/shard_map/kcab,ckl->lab/dot_general | solution.py:78
  107.6 5.3 %shard_map.40 = bf16[1,48,4,32,201]{4,3,2,1,0:T(8,128)(2,1)} custom-call(bf16[2,4,12,4,32,201]{5,4,3,2,1,0:T(8,128)(2,1)} %get-tuple-element.8.values_ref), custom_call_target="tpu_custom_call" | custom-call | tf_op jit(solution)/shard_map/pallas_call | solution.py:49
  112.9 4.8 %copy.23 = bf16[48,128,201,1]{1,0,3,2:T(8,128)(2,1)} copy(bf16[48,128,201,1]{2,1,0,3:T(8,128)(2,1)} %bitcast.58) | data formatting | bytes 4939776 | tf_op jit(solution)/shard_map/squeeze;reshape | solution.py:311
  117.7 2.7 %fusion.16 = bf16[201,2,32,128]{3,2,1,0:T(8,128)(2,1)S(1)} fusion(bf16[2,48,32,201]{1,2,0,3:T(8,128)(2,1)S(1)} %copy.18, bf16[48,128,201,1]{1,0,3,2:T(8,128)(2,1)} %copy.23), kind=kOutput, calls=%fused_computation.35 | convolution fusion | flops 158072832 | bytes 6998016 | tf_op jit(solution)/shard_map/cwak,wbk->kcab/dot_general | solution.py:75
  120.4 0.0 copy-start
  120.4 2.1 %fusion.4 = bf16[1,101,32,128]{3,1,2,0:T(8,128)(2,1)S(1)} fusion(bf16[201,2,32,128]{3,2,1,0:T(8,128)(2,1)S(1)} %fusion.16, bf16[2,201,101]{2,1,0:T(8,128)(2,1)S(1)} %convert_element_type.33), kind=kOutput, calls=%fused_computation.11 | convolution fusion | flops 333025280 | bytes 4201780 | tf_op jit(solution)/shard_map/kcab,ckl->lab/dot_general | solution.py:78
  122.6 0.0 copy-done
  122.6 0.2 maximum_bitcast_fusion
  122.8 1.4 %copy.12 = bf16[2,32,101,128]{3,1,2,0:T(8,128)(2,1)} copy(bf16[2,32,101,128]{3,2,1,0:T(8,128)(2,1)S(1)} %maximum_bitcast_fusion) | data formatting | bytes 3309568 | tf_op jit(solution)/shard_map/transpose | solution.py:313
  (5 shorter events, 0.1 us)
Async XLA Ops:
  120.4 2.2 %copy-start = (bf16[1,101,32,128]{3,1,2,0:T(8,128)(2,1)S(1)}, bf16[1,101,32,128]{3,1,2,0:T(8,128)(2,1)}, u32[]{:S(2)}) copy-start(bf16[1,101,32,128]{3,1,2,0:T(8,128)(2,1)} %fusion.3) | copy-start | bytes 2482180

commit v2 on v1

--- a/solution.py
+++ b/solution.py
@@ -17,14 +17,13 @@
 tile_rows = 8
 
 
-def whiten_kernel(values_ref, out_ref):
-    n_win, rows, _, _, nbins = values_ref.shape[1:]
-    half = rows // 2
+def whiten_into(piece, store, n_win, rows):
     power = None
     for win in range(n_win):
-        value_array = values_ref[0, win, :, 0].astype(jnp.float32)
+        value_array = piece(win).astype(jnp.float32)
         part = jnp.sum(value_array * value_array, axis=0)
         power = part if power is None else power + part
+    nbins = power.shape[1]
     padding = jnp.zeros((power.shape[0], half_band), jnp.float32)
     padded = jnp.concatenate([padding, power, padding], axis=1)
     total = padded[:, 0:nbins]
@@ -32,30 +31,10 @@
         total = total + padded[:, offset : offset + nbins]
     place = lax.broadcasted_iota(jnp.int32, power.shape, 1)
     count = 1 + jnp.minimum(place, half_band) + jnp.minimum(nbins - 1 - place, half_band)
-    windows = n_win * rows // 2
-    level = total / (count.astype(jnp.float32) * windows)
+    level = total / (count.astype(jnp.float32) * (n_win * rows // 2))
     scale = lax.rsqrt(level + eps_power)
     for win in range(n_win):
-        value_array = values_ref[0, win, :, 0].astype(jnp.float32)
-        white = (value_array * scale).astype(out_ref.dtype)
-        out_ref[0, pl.ds(win * rows, rows), 0] = white
-        if out_ref.shape[0] == 2:
-            out_ref[1, pl.ds(win * rows, half), 0] = white[half:]
-            out_ref[1, pl.ds(win * rows + half, half), 0] = -white[:half]
-
-
-def whiten_all(values, index, forms):
-    _, n_win, rows, shards, per_peer, nbins = values.shape
-    out = pl.pallas_call(
-        whiten_kernel,
-        grid=(shards,),
-        out_shape=jax.ShapeDtypeStruct((forms, n_win * rows, shards, per_peer, nbins), values.dtype),
-        in_specs=[
-            pl.BlockSpec((1, n_win, rows, 1, per_peer, nbins), lambda s: (index, 0, 0, s, 0, 0))
-        ],
-        out_specs=pl.BlockSpec((forms, n_win * rows, 1, per_peer, nbins), lambda s: (0, 0, s, 0, 0)),
-    )(values)
-    return out.reshape(forms, n_win * rows, shards * per_peer, nbins)
+        store(win, (piece(win).astype(jnp.float32) * scale).astype(jnp.bfloat16))
 
 
 def lag_table(nbins, nlags, windows):
@@ -85,9 +64,11 @@
 
 
 def exchange_kernel(
-    n_blk, n_win, pair_ref, own_ref, got_ref, src_ref, pair_stage, own_stage,
-    pair_send, pair_recv, pass_send, pass_recv, own_send, own_recv, local_sem
+    n_blk, n_win, rounds, pair_ref, own_ref, *refs
 ):
+    right_refs = refs[:rounds]
+    both_ref, got_ref, src_ref, pair_send, pair_recv = refs[rounds : rounds + 5]
+    pass_send, pass_recv, own_send, own_recv, local_sem = refs[rounds + 5 :]
     blk = lax.axis_index("blk")
     win = lax.axis_index("win")
     per_share = n_blk // n_win
@@ -148,19 +129,22 @@
             source, target, pass_send.at[mark, step], pass_recv.at[mark, step], blk, flip(win, over)
         )
 
-    stage_in = pltpu.make_async_copy(pair_ref.at[:, :, blk], pair_stage, local_sem.at[0])
-    stage_in.start()
+    rows = pair_ref.shape[1]
+    half = rows // 2
+    keep = pltpu.make_async_copy(
+        pair_ref.at[:, :, blk], got_ref.at[:, win, :, blk], local_sem.at[0]
+    )
+    keep.start()
     is_user = user == win
 
-    def own_in():
-        return pltpu.make_async_copy(own_ref.at[:, blk], own_stage, local_sem.at[1])
-
-    def own_out():
-        return pltpu.make_async_copy(own_stage, src_ref.at[win, :, place], local_sem.at[2])
+    def own_keep():
+        return pltpu.make_async_copy(
+            own_ref.at[:, blk], src_ref.at[win, :, place], local_sem.at[1]
+        )
 
     @pl.when(is_user)
     def _():
-        own_in().start()
+        own_keep().start()
 
     passes = []
     held = [0]
@@ -187,14 +171,11 @@
     def _():
         own(0).start()
 
-    stage_in.wait()
-    stage_out = pltpu.make_async_copy(pair_stage, got_ref.at[:, win, :, blk], local_sem.at[3])
-    stage_out.start()
+    keep.wait()
 
     @pl.when(is_user)
     def _():
-        own_in().wait()
-        own_out().start()
+        own_keep().wait()
 
     waited = set()
 
@@ -208,6 +189,18 @@
         else:
             over = offset & -offset
             passed(step, offset - over, over).wait_recv()
+
+    def finish(step):
+        for offset in held:
+            arrive(step, offset)
+        origin = (blk + n_blk - step) % n_blk
+
+        for index in range(rounds):
+
+            def store(peer, white):
+                right_refs[index][pl.ds(peer * rows, rows), origin] = white
+
+            whiten_into(lambda peer: got_ref[index, peer, :, origin], store, n_win, rows)
 
     for step in range(n_blk + 1):
         if 1 <= step < n_blk:
@@ -224,10 +217,9 @@
                     copy = passed(step - 1, offset, over)
                     copy.start()
                     sends.append(copy)
-    for step in range(n_blk):
-        for offset in held:
-            arrive(step, offset)
-
+        if step >= 2:
+            finish(step - 2)
+    finish(n_blk - 1)
     for local in range(per_share):
         for peer in range(n_win):
             here = jnp.logical_and(blk == win * per_share + local, win == peer)
@@ -239,18 +231,23 @@
                     piece, piece, own_send.at[0], own_recv.at[local * n_win + peer], blk, win
                 ).wait_recv()
 
+    def one_shard(local, carry):
+        def store(peer, white):
+            both_ref[0, pl.ds(peer * rows, rows), local] = white
+            both_ref[1, pl.ds(peer * rows, half), local] = white[half:]
+            both_ref[1, pl.ds(peer * rows + half, half), local] = -white[:half]
+
+        whiten_into(lambda peer: src_ref[peer, :, local], store, n_win, rows)
+        return carry
+
+    lax.fori_loop(0, per_share, one_shard, 0)
+
     for copy in sends:
         copy.wait_send()
 
     @pl.when(jnp.logical_not(is_user))
     def _():
         own(0).wait_send()
-
-    stage_out.wait()
-
-    @pl.when(is_user)
-    def _():
-        own_out().wait()
 
 
 def exchange(pair, own, n_blk, n_win):
@@ -258,24 +255,26 @@
     per_share = n_blk // n_win
     dtype = pair.dtype
     anywhere = pl.BlockSpec(memory_space=pl.ANY)
+    vmem = pl.BlockSpec(memory_space=pltpu.VMEM)
+    depth = n_win * rows
     return pl.pallas_call(
-        functools.partial(exchange_kernel, n_blk, n_win),
+        functools.partial(exchange_kernel, n_blk, n_win, rounds),
         out_shape=(
-            jax.ShapeDtypeStruct((rounds, n_win, rows, n_blk, per_peer, nbins), dtype),
-            jax.ShapeDtypeStruct((n_win, rows, per_share, per_peer, nbins), dtype),
+            *[jax.ShapeDtypeStruct((depth, n_blk, per_peer, nbins), dtype)] * rounds,
+            jax.ShapeDtypeStruct((2, depth, per_share, per_peer, nbins), dtype),
         ),
         in_specs=[anywhere, anywhere],
-        out_specs=(anywhere, anywhere),
+        out_specs=(vmem,) * (rounds + 1),
         scratch_shapes=[
-            pltpu.VMEM((rounds, rows, per_peer, nbins), dtype),
-            pltpu.VMEM((rows, per_peer, nbins), dtype),
+            pltpu.VMEM((rounds, n_win, rows, n_blk, per_peer, nbins), dtype),
+            pltpu.VMEM((n_win, rows, per_share, per_peer, nbins), dtype),
             pltpu.SemaphoreType.DMA((n_blk,)),
             pltpu.SemaphoreType.DMA((n_blk,)),
             pltpu.SemaphoreType.DMA((n_win - 1, n_blk)),
             pltpu.SemaphoreType.DMA((n_win - 1, n_blk)),
             pltpu.SemaphoreType.DMA((n_blk,)),
             pltpu.SemaphoreType.DMA((n_blk,)),
-            pltpu.SemaphoreType.DMA((4,)),
+            pltpu.SemaphoreType.DMA((2,)),
         ],
         compiler_params=pltpu.CompilerParams(collective_id=0, has_side_effects=True),
     )(pair, own)
@@ -304,12 +303,11 @@
     own = jnp.einsum(
         "zqc,xcf->xzqf", selector[ROUNDS], flat, preferred_element_type=jnp.float32
     ).astype(jnp.bfloat16)
-    got, mine_all = exchange(pair, own, n_blk, n_win)
-    both = whiten_all(mine_all[None], 0, 2)
+    *right, both = exchange(pair, own, n_blk, n_win)
+    right = [each.reshape(n_win * rows, chans, nbins) for each in right]
+    both = both.reshape(2, n_win * rows, share, nbins)
     table = lag_table(nbins, L, windows).reshape(2, nbins, L).astype(jnp.bfloat16)
-    results = [
-        correlate(both, whiten_all(got, index, 1)[0], table) for index in range(ROUNDS)
-    ]
+    results = [correlate(both, right[index], table) for index in range(ROUNDS)]
     return jnp.stack(results, axis=0).transpose(0, 2, 1, 3)
 
 

time: 125 us -> 115 us (0.920)
  Pallas kernels: 85.8 us -> 76.1 us
    reshape x1 -> x3, local copies, waits for them, and re-layouts: 6.53 us -> 16.4 us  [the longest x2 9.69 us: body(): right = [each.reshape(n_win * rows, chans, nbins) for each in right]]
    pallas_call x4 -> x1, Pallas kernels: 85.8 us -> 76.1 us  [exchange(): pl.pallas_call(functools.partial(exchange_kernel, n_blk, n_win, rounds),...]
    another operation x2 -> x0, local copies, waits for them, and re-layouts: 9.57 us -> none  [body(): whiten_all(got, index, 1)[0]]
where the time goes in v2:
time: 115 us
  Pallas kernels  76.1 us (66%)
  local copies, waits for them, and re-layouts  19 us (17%)
  matrix products  17.4 us (15%)
  other arithmetic  2.21 us (2%)
    pallas_call x1, Pallas kernels, exchange(): pl.pallas_call(functools.partial(exchange_kernel, n_blk, n_win, rounds),...  76.1 us
    reshape x2, local copies, waits for them, and re-layouts, body(): right = [each.reshape(n_win * rows, chans, nbins) for each in right]  9.69 us
    dot_general x2, matrix products, correlate(): jnp.einsum('kcab,ckl->lab', cross, table, preferred_element_type=jnp.floa...  7.1 us
    dot_general x2, matrix products, correlate(): jnp.einsum('cwak,wbk->kcab', both, right, preferred_element_type=jnp.floa...  7.05 us
    reshape x1, local copies, waits for them, and re-layouts, body(): both = both.reshape(2, n_win * rows, share, nbins)  6.72 us

profile of v2, /device:TPU:25, one launch (start us, length us, event | category | flops | bytes accessed | tf_op | source)
XLA Modules:
  0.0 114.8 jit_solution(6631897444600571728)
XLA Ops:
  0.0 1.2 %copy.7 = bf16[2,6,128,201]{2,3,1,0:T(8,128)(2,1)S(1)} copy(bf16[2,6,128,201]{2,0,3,1:T(2,128)(2,1)} %param.3) | data formatting | bytes 1234944 | tf_op args[0]
  1.2 0.7 fusion.13
  1.9 0.1 iota_add_fusion
  1.9 0.8 broadcast_compare_fusion
  2.7 1.7 %fusion.2.pair_ref = bf16[2,12,4,32,201]{4,3,2,1,0:T(8,128)(2,1)} fusion(bf16[12,128,201,1,1]{1,2,4,0,3:T(8,128)(2,1)S(1)} %bitcast.57, pred[3,4,32,128]{3,2,1,0:T(32,128)(4,1)S(1)} %broadcast_compare_fusion), kind=kOutput, calls=%fused_computation.8 | convolution fusion | flops 158690304 | bytes 1906688 | tf_op jit(solution)/shard_map/tzqc,xcf->txzqf/dot_general | solution.py:300
  4.5 1.6 %fusion.5.own_ref = bf16[12,4,32,201]{3,2,1,0:T(8,128)(2,1)} fusion(bf16[12,128,201,1]{1,2,3,0:T(8,128)(2,1)S(1)} %bitcast.58, pred[3,4,32,128]{3,2,1,0:T(32,128)(4,1)S(1)} %broadcast_compare_fusion), kind=kOutput, calls=%fused_computation.12 | convolution fusion | flops 79345152 | bytes 1272832 | tf_op jit(solution)/shard_map/zqc,xcf->xzqf/dot_general | solution.py:303
  6.0 76.1 %shard_map.37 = (bf16[48,4,32,201]{3,2,1,0:T(8,128)(2,1)}, bf16[48,4,32,201]{3,2,1,0:T(8,128)(2,1)}, bf16[2,48,1,32,201]{4,3,2,1,0:T(8,128)(2,1)}) custom-call(bf16[2,12,4,32,201]{4,3,2,1,0:T(8,128)(2,1)} %fusion.2.pair_ref, bf16[12,4,32,201]{3,2,1,0:T(8,128)(2,1)} %fusion.5.own_ref), custom_call_target="tpu_custom_call" | custom-call | tf_op jit(solution)/shard_map/pallas_call | solution.py:260
  82.1 6.7 %copy.18 = bf16[2,48,32,201]{1,2,0,3:T(8,128)(2,1)S(1)} copy(bf16[2,48,32,201]{3,2,1,0:T(8,128)(2,1)} %bitcast.61) | data formatting | bytes 2469888 | tf_op jit(solution)/shard_map/reshape | solution.py:308
  88.8 4.9 %copy.19 = bf16[48,128,201,1]{1,0,3,2:T(8,128)(2,1)} copy(bf16[48,128,201,1]{2,1,0,3:T(8,128)(2,1)} %bitcast.60) | data formatting | bytes 4939776 | tf_op jit(solution)/shard_map/reshape | solution.py:307
  93.7 4.4 %fusion.15 = bf16[201,2,32,128]{3,2,1,0:T(8,128)(2,1)} fusion(bf16[2,48,32,201]{1,2,0,3:T(8,128)(2,1)S(1)} %copy.18, bf16[48,128,201,1]{1,0,3,2:T(8,128)(2,1)} %copy.19), kind=kOutput, calls=%fused_computation.34 | convolution fusion | flops 158072832 | bytes 6998016 | tf_op jit(solution)/shard_map/cwak,wbk->kcab/dot_general | solution.py:54
  98.1 0.5 multiply_convert_fusion.1
  98.6 5.0 %fusion.3 = bf16[1,101,32,128]{3,1,2,0:T(8,128)(2,1)} fusion(bf16[201,2,32,128]{3,2,1,0:T(8,128)(2,1)} %fusion.15, bf16[2,201,101]{2,1,0:T(8,128)(2,1)S(1)} %convert_element_type.33), kind=kOutput, calls=%fused_computation.10 | convolution fusion | flops 333025280 | bytes 4201780 | tf_op jit(solution)/shard_map/kcab,ckl->lab/dot_general | solution.py:57
  103.6 4.8 %copy.23 = bf16[48,128,201,1]{1,0,3,2:T(8,128)(2,1)} copy(bf16[48,128,201,1]{2,1,0,3:T(8,128)(2,1)} %bitcast.59) | data formatting | bytes 4939776 | tf_op jit(solution)/shard_map/reshape | solution.py:307
  108.4 2.7 %fusion.16 = bf16[201,2,32,128]{3,2,1,0:T(8,128)(2,1)S(1)} fusion(bf16[2,48,32,201]{1,2,0,3:T(8,128)(2,1)S(1)} %copy.18, bf16[48,128,201,1]{1,0,3,2:T(8,128)(2,1)} %copy.23), kind=kOutput, calls=%fused_computation.35 | convolution fusion | flops 158072832 | bytes 6998016 | tf_op jit(solution)/shard_map/cwak,wbk->kcab/dot_general | solution.py:54
  111.1 0.0 copy-start
  111.1 2.1 %fusion.4 = bf16[1,101,32,128]{3,1,2,0:T(8,128)(2,1)S(1)} fusion(bf16[201,2,32,128]{3,2,1,0:T(8,128)(2,1)S(1)} %fusion.16, bf16[2,201,101]{2,1,0:T(8,128)(2,1)S(1)} %convert_element_type.33), kind=kOutput, calls=%fused_computation.11 | convolution fusion | flops 333025280 | bytes 4201780 | tf_op jit(solution)/shard_map/kcab,ckl->lab/dot_general | solution.py:57
  113.2 0.0 copy-done
  113.2 0.2 maximum_bitcast_fusion
  113.4 1.4 %copy.12 = bf16[2,32,101,128]{3,1,2,0:T(8,128)(2,1)} copy(bf16[2,32,101,128]{3,2,1,0:T(8,128)(2,1)S(1)} %maximum_bitcast_fusion) | data formatting | bytes 3309568 | tf_op jit(solution)/shard_map/transpose | solution.py:311
  (5 shorter events, 0.1 us)
Async XLA Ops:
  111.1 2.2 %copy-start = (bf16[1,101,32,128]{3,1,2,0:T(8,128)(2,1)S(1)}, bf16[1,101,32,128]{3,1,2,0:T(8,128)(2,1)}, u32[]{:S(2)}) copy-start(bf16[1,101,32,128]{3,1,2,0:T(8,128)(2,1)} %fusion.3) | copy-start | bytes 2482180

commit v3 on v2

--- a/solution.py
+++ b/solution.py
@@ -99,8 +99,18 @@
         bits.append(bit)
         bit //= 2
 
+    order = [0] + list(range(n_blk - 1, 0, -1))
+
+    def across(step):
+        other, each = blk, 1
+        while each < n_blk:
+            if step & each:
+                other = flip(other, each)
+            each *= 2
+        return other
+
     def direct(step):
-        dest = (blk + step) % n_blk
+        dest = across(step)
         return remote(
             pair_ref.at[:, :, dest], got_ref.at[:, win, :, blk],
             pair_send.at[step], pair_recv.at[step], dest, win,
@@ -110,14 +120,14 @@
     place = blk % per_share
 
     def own(step):
-        dest = (blk + step) % n_blk
+        dest = across(step)
         return remote(
             own_ref.at[:, dest], src_ref.at[win, :, place],
             own_send.at[step], own_recv.at[place * n_win + win], dest, user,
         )
 
     def passed(step, offset, over):
-        origin = (blk + n_blk - step) % n_blk
+        origin = across(step)
         slot = win
         for each in bits:
             if offset & each:
@@ -158,11 +168,11 @@
             copy = passed(0, 0, over)
             copy.start()
             sends.append(copy)
-    for step in range(1, n_blk):
+    for step in order[1:]:
         copy = direct(step)
         copy.start()
         sends.append(copy)
-    for step in range(1, n_blk):
+    for step in order[1:]:
         copy = own(step)
         copy.start()
         sends.append(copy)
@@ -193,7 +203,7 @@
     def finish(step):
         for offset in held:
             arrive(step, offset)
-        origin = (blk + n_blk - step) % n_blk
+        origin = across(step)
 
         for index in range(rounds):
 
@@ -202,24 +212,26 @@
 
             whiten_into(lambda peer: got_ref[index, peer, :, origin], store, n_win, rows)
 
-    for step in range(n_blk + 1):
-        if 1 <= step < n_blk:
+    for turn in range(n_blk + 1):
+        if 1 <= turn < n_blk:
+            step = order[turn]
             arrive(step, 0)
             for offset, over in passes:
                 if offset == 0:
                     copy = passed(step, 0, over)
                     copy.start()
                     sends.append(copy)
-        if step >= 1:
+        if turn >= 1:
+            step = order[turn - 1]
             for offset, over in passes:
                 if offset:
-                    arrive(step - 1, offset)
-                    copy = passed(step - 1, offset, over)
+                    arrive(step, offset)
+                    copy = passed(step, offset, over)
                     copy.start()
                     sends.append(copy)
-        if step >= 2:
-            finish(step - 2)
-    finish(n_blk - 1)
+        if turn >= 2:
+            finish(order[turn - 2])
+    finish(order[n_blk - 1])
     for local in range(per_share):
         for peer in range(n_win):
             here = jnp.logical_and(blk == win * per_share + local, win == peer)

time: 115 us -> 117 us (1.017); the launches traced: 115 us -> 115 us
  no operation moved by 1% of the time
where the time goes in v3:
time: 117 us; the launch traced here: 115 us
  Pallas kernels  76.1 us (65%)
  local copies, waits for them, and re-layouts  19 us (16%)
  matrix products  17.4 us (15%)
  other arithmetic  2.21 us (2%)
    pallas_call x1, Pallas kernels, exchange(): pl.pallas_call(functools.partial(exchange_kernel, n_blk, n_win, rounds),...  76.1 us
    reshape x2, local copies, waits for them, and re-layouts, body(): right = [each.reshape(n_win * rows, chans, nbins) for each in right]  9.69 us
    dot_general x2, matrix products, correlate(): jnp.einsum('kcab,ckl->lab', cross, table, preferred_element_type=jnp.floa...  7.09 us
    dot_general x2, matrix products, correlate(): jnp.einsum('cwak,wbk->kcab', both, right, preferred_element_type=jnp.floa...  7.05 us
    reshape x1, local copies, waits for them, and re-layouts, body(): both = both.reshape(2, n_win * rows, share, nbins)  6.72 us

profile of v3, /device:TPU:25, one launch (start us, length us, event | category | flops | bytes accessed | tf_op | source)
XLA Modules:
  0.0 114.8 jit_solution(7634796481674780469)
XLA Ops:
  0.0 1.2 %copy.7 = bf16[2,6,128,201]{2,3,1,0:T(8,128)(2,1)S(1)} copy(bf16[2,6,128,201]{2,0,3,1:T(2,128)(2,1)} %param.3) | data formatting | bytes 1234944 | tf_op args[0]
  1.2 0.7 fusion.13
  1.9 0.1 iota_add_fusion
  1.9 0.8 broadcast_compare_fusion
  2.7 1.7 %fusion.2.pair_ref = bf16[2,12,4,32,201]{4,3,2,1,0:T(8,128)(2,1)} fusion(bf16[12,128,201,1,1]{1,2,4,0,3:T(8,128)(2,1)S(1)} %bitcast.57, pred[3,4,32,128]{3,2,1,0:T(32,128)(4,1)S(1)} %broadcast_compare_fusion), kind=kOutput, calls=%fused_computation.8 | convolution fusion | flops 158690304 | bytes 1906688 | tf_op jit(solution)/shard_map/tzqc,xcf->txzqf/dot_general | solution.py:312
  4.5 1.6 %fusion.5.own_ref = bf16[12,4,32,201]{3,2,1,0:T(8,128)(2,1)} fusion(bf16[12,128,201,1]{1,2,3,0:T(8,128)(2,1)S(1)} %bitcast.58, pred[3,4,32,128]{3,2,1,0:T(32,128)(4,1)S(1)} %broadcast_compare_fusion), kind=kOutput, calls=%fused_computation.12 | convolution fusion | flops 79345152 | bytes 1272832 | tf_op jit(solution)/shard_map/zqc,xcf->xzqf/dot_general | solution.py:315
  6.0 76.1 %shard_map.37 = (bf16[48,4,32,201]{3,2,1,0:T(8,128)(2,1)}, bf16[48,4,32,201]{3,2,1,0:T(8,128)(2,1)}, bf16[2,48,1,32,201]{4,3,2,1,0:T(8,128)(2,1)}) custom-call(bf16[2,12,4,32,201]{4,3,2,1,0:T(8,128)(2,1)} %fusion.2.pair_ref, bf16[12,4,32,201]{3,2,1,0:T(8,128)(2,1)} %fusion.5.own_ref), custom_call_target="tpu_custom_call" | custom-call | tf_op jit(solution)/shard_map/pallas_call | solution.py:272
  82.1 6.7 %copy.18 = bf16[2,48,32,201]{1,2,0,3:T(8,128)(2,1)S(1)} copy(bf16[2,48,32,201]{3,2,1,0:T(8,128)(2,1)} %bitcast.61) | data formatting | bytes 2469888 | tf_op jit(solution)/shard_map/reshape | solution.py:320
  88.8 4.9 %copy.19 = bf16[48,128,201,1]{1,0,3,2:T(8,128)(2,1)} copy(bf16[48,128,201,1]{2,1,0,3:T(8,128)(2,1)} %bitcast.60) | data formatting | bytes 4939776 | tf_op jit(solution)/shard_map/reshape | solution.py:319
  93.7 4.4 %fusion.15 = bf16[201,2,32,128]{3,2,1,0:T(8,128)(2,1)} fusion(bf16[2,48,32,201]{1,2,0,3:T(8,128)(2,1)S(1)} %copy.18, bf16[48,128,201,1]{1,0,3,2:T(8,128)(2,1)} %copy.19), kind=kOutput, calls=%fused_computation.34 | convolution fusion | flops 158072832 | bytes 6998016 | tf_op jit(solution)/shard_map/cwak,wbk->kcab/dot_general | solution.py:54
  98.1 0.5 multiply_convert_fusion.1
  98.6 5.0 %fusion.3 = bf16[1,101,32,128]{3,1,2,0:T(8,128)(2,1)} fusion(bf16[201,2,32,128]{3,2,1,0:T(8,128)(2,1)} %fusion.15, bf16[2,201,101]{2,1,0:T(8,128)(2,1)S(1)} %convert_element_type.33), kind=kOutput, calls=%fused_computation.10 | convolution fusion | flops 333025280 | bytes 4201780 | tf_op jit(solution)/shard_map/kcab,ckl->lab/dot_general | solution.py:57
  103.6 4.8 %copy.23 = bf16[48,128,201,1]{1,0,3,2:T(8,128)(2,1)} copy(bf16[48,128,201,1]{2,1,0,3:T(8,128)(2,1)} %bitcast.59) | data formatting | bytes 4939776 | tf_op jit(solution)/shard_map/reshape | solution.py:319
  108.4 2.7 %fusion.16 = bf16[201,2,32,128]{3,2,1,0:T(8,128)(2,1)S(1)} fusion(bf16[2,48,32,201]{1,2,0,3:T(8,128)(2,1)S(1)} %copy.18, bf16[48,128,201,1]{1,0,3,2:T(8,128)(2,1)} %copy.23), kind=kOutput, calls=%fused_computation.35 | convolution fusion | flops 158072832 | bytes 6998016 | tf_op jit(solution)/shard_map/cwak,wbk->kcab/dot_general | solution.py:54
  111.1 0.0 copy-start
  111.1 2.1 %fusion.4 = bf16[1,101,32,128]{3,1,2,0:T(8,128)(2,1)S(1)} fusion(bf16[201,2,32,128]{3,2,1,0:T(8,128)(2,1)S(1)} %fusion.16, bf16[2,201,101]{2,1,0:T(8,128)(2,1)S(1)} %convert_element_type.33), kind=kOutput, calls=%fused_computation.11 | convolution fusion | flops 333025280 | bytes 4201780 | tf_op jit(solution)/shard_map/kcab,ckl->lab/dot_general | solution.py:57
  113.2 0.0 copy-done
  113.2 0.2 maximum_bitcast_fusion
  113.4 1.4 %copy.12 = bf16[2,32,101,128]{3,1,2,0:T(8,128)(2,1)} copy(bf16[2,32,101,128]{3,2,1,0:T(8,128)(2,1)S(1)} %maximum_bitcast_fusion) | data formatting | bytes 3309568 | tf_op jit(solution)/shard_map/transpose | solution.py:323
  (5 shorter events, 0.1 us)
Async XLA Ops:
  111.1 2.2 %copy-start = (bf16[1,101,32,128]{3,1,2,0:T(8,128)(2,1)S(1)}, bf16[1,101,32,128]{3,1,2,0:T(8,128)(2,1)}, u32[]{:S(2)}) copy-start(bf16[1,101,32,128]{3,1,2,0:T(8,128)(2,1)} %fusion.3) | copy-start | bytes 2482180

commit v4 on v3

--- a/solution.py
+++ b/solution.py
@@ -99,7 +99,7 @@
         bits.append(bit)
         bit //= 2
 
-    order = [0] + list(range(n_blk - 1, 0, -1))
+    order = list(range(n_blk))
 
     def across(step):
         other, each = blk, 1

time: 117 us -> 107 us (0.915)
  the two profiles are of different devices: /device:TPU:25 before, /device:TPU:11 now
where the time goes in v4:
time: 107 us
  Pallas kernels  67.9 us (63%)
  local copies, waits for them, and re-layouts  19 us (18%)
  matrix products  17.4 us (16%)
  other arithmetic  2.21 us (2%)
    pallas_call x1, Pallas kernels, exchange(): pl.pallas_call(functools.partial(exchange_kernel, n_blk, n_win, rounds),...  67.9 us
    reshape x2, local copies, waits for them, and re-layouts, body(): right = [each.reshape(n_win * rows, chans, nbins) for each in right]  9.69 us
    dot_general x2, matrix products, correlate(): jnp.einsum('kcab,ckl->lab', cross, table, preferred_element_type=jnp.floa...  7.1 us
    dot_general x2, matrix products, correlate(): jnp.einsum('cwak,wbk->kcab', both, right, preferred_element_type=jnp.floa...  7.05 us
    reshape x1, local copies, waits for them, and re-layouts, body(): both = both.reshape(2, n_win * rows, share, nbins)  6.72 us

profile of v4, /device:TPU:11, one launch (start us, length us, event | category | flops | bytes accessed | tf_op | source)
XLA Modules:
  0.0 106.7 jit_solution(215818624461247546)
XLA Ops:
  0.0 1.2 %copy.7 = bf16[2,6,128,201]{2,3,1,0:T(8,128)(2,1)S(1)} copy(bf16[2,6,128,201]{2,0,3,1:T(2,128)(2,1)} %param.3) | data formatting | bytes 1234944 | tf_op args[0]
  1.2 0.7 fusion.13
  1.9 0.1 iota_add_fusion
  1.9 0.8 broadcast_compare_fusion
  2.7 1.7 %fusion.2.pair_ref = bf16[2,12,4,32,201]{4,3,2,1,0:T(8,128)(2,1)} fusion(bf16[12,128,201,1,1]{1,2,4,0,3:T(8,128)(2,1)S(1)} %bitcast.57, pred[3,4,32,128]{3,2,1,0:T(32,128)(4,1)S(1)} %broadcast_compare_fusion), kind=kOutput, calls=%fused_computation.8 | convolution fusion | flops 158690304 | bytes 1906688 | tf_op jit(solution)/shard_map/tzqc,xcf->txzqf/dot_general | solution.py:312
  4.5 1.6 %fusion.5.own_ref = bf16[12,4,32,201]{3,2,1,0:T(8,128)(2,1)} fusion(bf16[12,128,201,1]{1,2,3,0:T(8,128)(2,1)S(1)} %bitcast.58, pred[3,4,32,128]{3,2,1,0:T(32,128)(4,1)S(1)} %broadcast_compare_fusion), kind=kOutput, calls=%fused_computation.12 | convolution fusion | flops 79345152 | bytes 1272832 | tf_op jit(solution)/shard_map/zqc,xcf->xzqf/dot_general | solution.py:315
  6.0 67.9 %shard_map.37 = (bf16[48,4,32,201]{3,2,1,0:T(8,128)(2,1)}, bf16[48,4,32,201]{3,2,1,0:T(8,128)(2,1)}, bf16[2,48,1,32,201]{4,3,2,1,0:T(8,128)(2,1)}) custom-call(bf16[2,12,4,32,201]{4,3,2,1,0:T(8,128)(2,1)} %fusion.2.pair_ref, bf16[12,4,32,201]{3,2,1,0:T(8,128)(2,1)} %fusion.5.own_ref), custom_call_target="tpu_custom_call" | custom-call | tf_op jit(solution)/shard_map/pallas_call | solution.py:272
  74.0 6.7 %copy.18 = bf16[2,48,32,201]{1,2,0,3:T(8,128)(2,1)S(1)} copy(bf16[2,48,32,201]{3,2,1,0:T(8,128)(2,1)} %bitcast.61) | data formatting | bytes 2469888 | tf_op jit(solution)/shard_map/reshape | solution.py:320
  80.7 4.9 %copy.19 = bf16[48,128,201,1]{1,0,3,2:T(8,128)(2,1)} copy(bf16[48,128,201,1]{2,1,0,3:T(8,128)(2,1)} %bitcast.60) | data formatting | bytes 4939776 | tf_op jit(solution)/shard_map/reshape | solution.py:319
  85.6 4.4 %fusion.15 = bf16[201,2,32,128]{3,2,1,0:T(8,128)(2,1)} fusion(bf16[2,48,32,201]{1,2,0,3:T(8,128)(2,1)S(1)} %copy.18, bf16[48,128,201,1]{1,0,3,2:T(8,128)(2,1)} %copy.19), kind=kOutput, calls=%fused_computation.34 | convolution fusion | flops 158072832 | bytes 6998016 | tf_op jit(solution)/shard_map/cwak,wbk->kcab/dot_general | solution.py:54
  89.9 0.5 multiply_convert_fusion.1
  90.5 5.0 %fusion.3 = bf16[1,101,32,128]{3,1,2,0:T(8,128)(2,1)} fusion(bf16[201,2,32,128]{3,2,1,0:T(8,128)(2,1)} %fusion.15, bf16[2,201,101]{2,1,0:T(8,128)(2,1)S(1)} %convert_element_type.33), kind=kOutput, calls=%fused_computation.10 | convolution fusion | flops 333025280 | bytes 4201780 | tf_op jit(solution)/shard_map/kcab,ckl->lab/dot_general | solution.py:57
  95.4 4.8 %copy.23 = bf16[48,128,201,1]{1,0,3,2:T(8,128)(2,1)} copy(bf16[48,128,201,1]{2,1,0,3:T(8,128)(2,1)} %bitcast.59) | data formatting | bytes 4939776 | tf_op jit(solution)/shard_map/reshape | solution.py:319
  100.2 2.7 %fusion.16 = bf16[201,2,32,128]{3,2,1,0:T(8,128)(2,1)S(1)} fusion(bf16[2,48,32,201]{1,2,0,3:T(8,128)(2,1)S(1)} %copy.18, bf16[48,128,201,1]{1,0,3,2:T(8,128)(2,1)} %copy.23), kind=kOutput, calls=%fused_computation.35 | convolution fusion | flops 158072832 | bytes 6998016 | tf_op jit(solution)/shard_map/cwak,wbk->kcab/dot_general | solution.py:54
  102.9 0.0 copy-start
  103.0 2.1 %fusion.4 = bf16[1,101,32,128]{3,1,2,0:T(8,128)(2,1)S(1)} fusion(bf16[201,2,32,128]{3,2,1,0:T(8,128)(2,1)S(1)} %fusion.16, bf16[2,201,101]{2,1,0:T(8,128)(2,1)S(1)} %convert_element_type.33), kind=kOutput, calls=%fused_computation.11 | convolution fusion | flops 333025280 | bytes 4201780 | tf_op jit(solution)/shard_map/kcab,ckl->lab/dot_general | solution.py:57
  105.1 0.0 copy-done
  105.1 0.2 maximum_bitcast_fusion
  105.3 1.4 %copy.12 = bf16[2,32,101,128]{3,1,2,0:T(8,128)(2,1)} copy(bf16[2,32,101,128]{3,2,1,0:T(8,128)(2,1)S(1)} %maximum_bitcast_fusion) | data formatting | bytes 3309568 | tf_op jit(solution)/shard_map/transpose | solution.py:323
  (5 shorter events, 0.1 us)
Async XLA Ops:
  102.9 2.2 %copy-start = (bf16[1,101,32,128]{3,1,2,0:T(8,128)(2,1)S(1)}, bf16[1,101,32,128]{3,1,2,0:T(8,128)(2,1)}, u32[]{:S(2)}) copy-start(bf16[1,101,32,128]{3,1,2,0:T(8,128)(2,1)} %fusion.3) | copy-start | bytes 2482180
